TPU v7x, 32 devices: a whole 2x2x4 slice. The times are simulated.
32 devices in a mesh: rows: 8 (over z, y), cols: 4 (over x, core).
Axes of the slice: x: 2, y: 2, z: 4, core: 2. Of those that a mesh axis runs over, the one named last changes fastest.
Arguments:
- feats_t: bfloat16 [128, 16384], P('cols', 'rows'), may hold values from -6 to 6
- adj_index: int32 [128, 16], replicated, may hold values from 0 to 127, as said below
- adj_weight: bfloat16 [128, 16, 128, 128], P('rows'), as said below
- weight: bfloat16 [128, 256], replicated, may hold values from -0.5 to 0.5
- cotangent_t: bfloat16 [256, 16384], P('cols', 'rows'), may hold values from -6 to 6
Outputs:
- output_t: bfloat16 [256, 16384], P('cols', 'rows')
- weight_grad: float32 [128, 256], P('cols')
- feat_grad: float32 [128, 16384], P('cols', 'rows')
Inputs may be any that keep to these rules, and one draw needn't show every extreme that they name: `adj_index`: slot 0 of row block i names block i itself. Blocks are grouped 16 to a device in order. Slot 1 names a block of the next device (device index plus one, cyclically). The row blocks of one device name at most 4 distinct blocks of any other device, and exactly 4 of the next one. A block may stand in several slots of one row block. `adj_weight`: Nonnegative; about one entry in eight is nonzero.
All inputs are finite; a program needn't handle non-finite values.
Results may differ from a plain program's by a relative error of at most 0.0054.
Values may be sent and summed in bfloat16 or wider, within the bound.
No kernel may reach another device: no remote copies, remote signals or barrier semaphores. Data moves between devices by JAX's collectives and lax.ppermute only.
A program may use at most 128 MiB of HBM per device.

v0:
```python
import math
import jax
import jax.numpy as jnp
from jax import lax
from jax.sharding import PartitionSpec as P

CAP = 4


def body(feats_t, adj_index, adj_weight, weight, cotangent_t):
    feat_rows, node_cols = feats_t.shape
    blocks_n = adj_weight.shape[0]
    slots_n = adj_weight.shape[1]
    tile_n = adj_weight.shape[2]
    row_devs = lax.axis_size("rows")
    row_pos = lax.axis_index("rows")
    col_pos = lax.axis_index("cols")
    unit_rows = cotangent_t.shape[0]
    own_index = lax.dynamic_slice_in_dim(adj_index, row_pos * blocks_n, blocks_n, 0)
    own_flat = own_index.reshape(-1)
    local_tiles = feats_t.reshape(feat_rows, blocks_n, tile_n).transpose(1, 0, 2)
    device_ids = jnp.arange(row_devs, dtype=jnp.int32)
    slot_ids = jnp.arange(CAP, dtype=jnp.int32)
    mine = row_pos * blocks_n + jnp.arange(blocks_n, dtype=jnp.int32)
    peers_index = adj_index.reshape(row_devs, blocks_n * slots_n)
    wanted = (
        jnp.any(peers_index[:, :, None] == mine[None, None, :], axis=1)
        & (device_ids != row_pos)[:, None]
    )
    ordinal = jnp.cumsum(wanted.astype(jnp.int32), axis=1) - 1
    selector = wanted[:, None, :] & (ordinal[:, None, :] == slot_ids[None, :, None])
    source = own_flat // blocks_n
    block_pos = own_flat % blocks_n
    needed = jnp.any(
        own_flat[:, None] == jnp.arange(row_devs * blocks_n, dtype=jnp.int32)[None, :], axis=0
    )
    needed = needed.reshape(row_devs, blocks_n) & (device_ids != row_pos)[:, None]
    need_order = jnp.cumsum(needed.astype(jnp.int32), axis=1) - 1
    slot_of = source * CAP + need_order.reshape(-1)[own_flat]
    remote = source != row_pos
    outgoing = jnp.einsum(
        "pcb,bfj->pcfj",
        selector.astype(jnp.bfloat16),
        local_tiles,
        preferred_element_type=jnp.float32,
    ).astype(jnp.bfloat16)
    incoming = lax.all_to_all(outgoing, "rows", split_axis=0, concat_axis=0, tiled=True)
    received = incoming.reshape(row_devs * CAP, feat_rows, tile_n)[slot_of]
    own_part = local_tiles[block_pos]
    picked = jnp.where(remote[:, None, None], received, own_part).reshape(
        blocks_n, slots_n, feat_rows, tile_n
    )
    aggregate = jnp.einsum("bkfj,bkij->fbi", picked, adj_weight, preferred_element_type=jnp.float32)
    aggregated = aggregate.reshape(feat_rows, node_cols).astype(jnp.bfloat16)
    w_slab = lax.dynamic_slice_in_dim(weight, col_pos * unit_rows, unit_rows, 1)
    pre_act = lax.dot_general(
        w_slab,
        lax.all_gather(aggregated, "cols", axis=0, tiled=True),
        (((0,), (0,)), ((), ())),
        preferred_element_type=jnp.float32,
    )
    output_t = jax.nn.silu(pre_act).astype(jnp.bfloat16)
    sigm = jax.nn.sigmoid(pre_act)
    pre_grad = (cotangent_t.astype(jnp.float32) * sigm * (1.0 + pre_act * (1.0 - sigm))).astype(
        jnp.bfloat16
    )
    w_mine = lax.dynamic_slice_in_dim(weight, col_pos * feat_rows, feat_rows, 0)
    portion = lax.all_gather(pre_grad, "cols", axis=0, tiled=True)
    grad_acc = jnp.dot(w_mine, portion, preferred_element_type=jnp.float32)
    block_grad = lax.dot_general(
        aggregated, portion, (((1,), (1,)), ((), ())), preferred_element_type=jnp.float32
    )
    grad_scale = 1.0 / math.sqrt(node_cols * row_devs)
    weight_grad = lax.psum(block_grad, "rows") * grad_scale
    agg_grad = grad_acc.astype(jnp.bfloat16)
    contrib = jnp.einsum(
        "fbi,bkij->bkfj",
        agg_grad.reshape(feat_rows, blocks_n, tile_n),
        adj_weight,
        preferred_element_type=jnp.float32,
    )
    contrib_flat = contrib.reshape(blocks_n * slots_n, feat_rows * tile_n)
    slot_total = row_devs * CAP
    send_target = jnp.where(remote, slot_of, slot_total)
    sending = jax.ops.segment_sum(contrib_flat, send_target, num_segments=slot_total + 1)[
        :slot_total
    ]
    sending = sending.reshape(row_devs, CAP, feat_rows, tile_n)
    arrived = lax.all_to_all(
        sending.astype(jnp.bfloat16), "rows", split_axis=0, concat_axis=0, tiled=True
    ).astype(sending.dtype)
    arrived_flat = arrived.reshape(slot_total, feat_rows * tile_n)
    block_ids = jnp.arange(blocks_n, dtype=jnp.int32)
    slot_block = jnp.sum(selector.astype(jnp.int32) * block_ids[None, None, :], axis=2)
    slot_used = jnp.any(selector, axis=2)
    peer_target = jnp.where(slot_used, slot_block, blocks_n).reshape(-1)
    from_peers = jax.ops.segment_sum(arrived_flat, peer_target, num_segments=blocks_n + 1)[
        :blocks_n
    ]
    self_target = jnp.where(remote, blocks_n, block_pos)
    from_self = jax.ops.segment_sum(contrib_flat, self_target, num_segments=blocks_n + 1)[:blocks_n]
    summed = (from_peers + from_self).reshape(blocks_n, feat_rows, tile_n)
    feat_grad = summed.transpose(1, 0, 2).reshape(feat_rows, node_cols)
    return (output_t, weight_grad, feat_grad)


def solution(mesh):
    return jax.shard_map(
        body,
        mesh=mesh,
        in_specs=(P("cols", "rows"), P(), P("rows", None, None, None), P(), P("cols", "rows")),
        out_specs=(P("cols", "rows"), P("cols", None), P("cols", "rows")),
        check_vma=False,
    )
```

profile of v0, /device:TPU:0, one launch (start us, length us, event | category | flops | bytes accessed | tf_op | source)
XLA Modules:
  0.0 143.8 jit_solution(9876244328487271256)
XLA Ops:
  7.2 0.8 copy.41
  8.0 0.8 fusion.39
  9.8 0.9 copy.60
  10.9 0.7 copy.44
  11.7 7.3 %all-to-all-start = ((bf16[8,4,32,128]{3,2,1,0:T(8,128)(2,1)}), bf16[8,4,32,128]{3,2,1,0:T(8,128)(2,1)S(1)}, u32[]{:S(2)}, u32[]{:S(2)}) async-start(bf16[8,4,32,128]{3,2,1,0:T(8,128)(2,1)} %copy.44), calls=%async_computation | async-start | bytes 524288 | tf_op jit(solution)/shard_map/all_to_all | solution.py:47
  19.4 1.9 %gather_fusion = s32[256]{0:T(256)S(1)} fusion(s32[128]{0:T(128)S(1)} %sub.23, s32[1024]{0:T(1024)S(1)} %pad_clamp_fusion.2), kind=kCustom, calls=%fused_computation | custom fusion | bytes 3072 | tf_op jit(solution)/shard_map/gather | solution.py:39
  21.4 0.9 bitcast_bitcast_fusion
  22.3 1.0 gather_fusion.2
  23.4 4.6 %all-to-all-done = bf16[8,4,32,128]{3,2,1,0:T(8,128)(2,1)S(1)} async-done(((bf16[8,4,32,128]{3,2,1,0:T(8,128)(2,1)}), bf16[8,4,32,128]{3,2,1,0:T(8,128)(2,1)S(1)}, u32[]{:S(2)}, u32[]{:S(2)}) %all-to-all-start) | async-done | bytes 262176 | tf_op jit(solution)/shard_map/all_to_all | solution.py:47
  27.9 2.2 %gather_fusion.1 = bf16[256,32,128]{2,1,0:T(8,128)(2,1)} fusion(bf16[32,32,128]{2,1,0:T(8,128)(2,1)S(1)} %bitcast.83, s32[1024]{0:T(1024)S(1)} %pad_clamp_fusion.1), kind=kCustom, calls=%fused_computation.1 | custom fusion | bytes 4195328 | tf_op jit(solution)/shard_map/gather | solution.py:48
  30.1 6.9 %fusion.16 = bf16[16,4,8,128]{3,2,1,0:T(8,128)(2,1)S(1)} fusion(bf16[16,16,128,128]{3,2,1,0:T(8,128)(2,1)} %param.7, bf16[16,16,32,128]{3,2,1,0:T(8,128)(2,1)} %bitcast.85, bf16[16,16,32,128]{3,2,1,0:T(8,128)(2,1)S(1)} %bitcast.84, pred[16,16]{1,0:T(8,128)(4,1)S(1)} %copy.40), kind=kOutput, calls=%fused_computation.20 | convolution fusion | flops 269549568 | bytes 12714240 | tf_op jit(solution)/shard_map/bkfj,bkij->fbi/dot_general | solution.py:53
  37.1 7.3 %all_gather.6 = bf16[128,2048]{1,0:T(8,128)(2,1)S(1)} all-gather(bf16[32,2048]{1,0:T(8,128)(2,1)S(1)} %bitcast.90), channel_id=1, replica_groups=mesh['rows'=8,'cols'=4] {'cols'}, dimensions={0}, use_global_device_ids=true | all-gather | bytes 655360 | tf_op jit(solution)/shard_map/all_gather | solution.py:58
  44.4 1.3 multiply_convert_fusion
  46.2 14.7 %all-gather.2.cloned.1.call-done = bf16[256,2048]{1,0:T(8,128)(2,1)} async-done(((bf16[64,2048]{1,0:T(8,128)(2,1)}), bf16[256,2048]{1,0:T(8,128)(2,1)}) %all-gather.2.cloned.1.call-update) | async-done | bytes 1048592 | tf_op jit(solution)/shard_map/all_gather | solution.py:68
  60.9 1.5 %fusion.15 = bf16[4,8,16,128]{3,1,2,0:T(8,128)(2,1)S(1)} fusion(bf16[256,2048]{1,0:T(8,128)(2,1)} %all-gather.2.cloned.1.call-done, bf16[128,256]{1,0:T(8,128)(2,1)S(1)} %copy-done, s32[]{:T(128)S(6)} %select_n.136), kind=kOutput, calls=%fused_computation.19 | convolution fusion | flops 33619968 | bytes 1196036 | tf_op jit(solution)/shard_map/dot_general | solution.py:69
  62.5 6.5 %fusion.28 = f32[16,32,16,128]{3,1,2,0:T(8,128)} fusion(bf16[16,16,128,128]{3,2,1,0:T(8,128)(2,1)} %param.7, bf16[32,16,128,1]{2,1,0,3:T(8,128)(2,1)S(1)} %bitcast.88), kind=kOutput, calls=%fused_computation.38 | convolution fusion | flops 268435456 | bytes 12713984 | tf_op jit(solution)/shard_map/fbi,bkij->bkfj/dot_general | solution.py:76
  69.0 10.2 %scatter_custom_fusion.2 = f32[17,4096]{1,0:T(8,128)S(1)} fusion(s32[256]{0:T(256)S(1)} %bitcast.99, f32[32,8,32,128]{3,2,1,0:T(8,128)} %bitcast.81, f32[]{:T(128)} %constant.69.clone.1), kind=kCustom, calls=%fused_computation.6 | custom fusion | flops 1048576 | bytes 4472836 | tf_op jit(solution)/shard_map/scatter-add | solution.py:101
  79.3 10.2 %scatter_custom_fusion = f32[33,4096]{1,0:T(8,128)S(1)} fusion(s32[256]{0:T(256)S(1)} %bitcast.98, f32[32,8,32,128]{3,2,1,0:T(8,128)} %bitcast.82, f32[]{:T(128)} %constant.69.clone.1), kind=kCustom, calls=%fused_computation.8 | custom fusion | flops 1048576 | bytes 4734980 | tf_op jit(solution)/shard_map/scatter-add | solution.py:85
  89.5 0.7 copy.63
  90.3 5.5 %all-to-all-start.1 = ((bf16[8,4,32,128]{3,2,1,0:T(8,128)(2,1)}), bf16[8,4,32,128]{3,2,1,0:T(8,128)(2,1)S(1)}, u32[]{:S(2)}, u32[]{:S(2)}) async-start(bf16[8,4,32,128]{3,2,1,0:T(8,128)(2,1)} %bitcast.37), calls=%async_computation.1 | async-start | bytes 524288 | tf_op jit(solution)/shard_map/all_to_all | solution.py:89
  96.2 37.6 %psum.7 = f32[32,256]{1,0:T(8,128)S(1)} all-reduce(f32[32,256]{1,0:T(8,128)S(1)} %fusion.45), channel_id=1, replica_groups=mesh['rows'=8,'cols'=4] {'rows'}, use_global_device_ids=true, to_apply=%region_4.5 | all-reduce | flops 8192 | bytes 65536 | tf_op jit(solution)/shard_map/psum | solution.py:74
  133.8 0.6 broadcast_multiply_fusion
  134.4 1.7 %scatter_custom_fusion.1 = f32[17,4096]{1,0:T(8,128)S(1)} fusion(s32[32]{0:T(128)S(1)} %reshape.376, f32[4,8,32,128]{3,2,1,0:T(8,128)S(1)} %bitcast_convert_fusion, f32[]{:T(128)} %constant.69.clone.1), kind=kCustom, calls=%fused_computation.21 | custom fusion | flops 131072 | bytes 802820 | tf_op jit(solution)/shard_map/scatter-add | solution.py:97
  136.2 0.7 copy.84
  (44 shorter events, 2.8 us)
Async XLA Ops:
  7.2 37.3 %copy-start = (bf16[128,256]{1,0:T(8,128)(2,1)S(1)}, bf16[128,256]{1,0:T(8,128)(2,1)}, u32[]{:S(2)}) copy-start(bf16[128,256]{1,0:T(8,128)(2,1)} %param.8) | copy-start | bytes 196612
  11.7 16.2 %all-to-all-start = ((bf16[8,4,32,128]{3,2,1,0:T(8,128)(2,1)}), bf16[8,4,32,128]{3,2,1,0:T(8,128)(2,1)S(1)}, u32[]{:S(2)}, u32[]{:S(2)}) async-start(bf16[8,4,32,128]{3,2,1,0:T(8,128)(2,1)} %copy.44), calls=%async_computation | async-start | bytes 524288 | tf_op jit(solution)/shard_map/all_to_all | solution.py:47
  19.0 41.9 %all-gather.2.cloned.1.call-start = ((), (), s32[]{:S(2)}) async-start(), calls=%async_computation.2 | async-start | bytes 1310720 | tf_op jit(solution)/shard_map/all_gather | solution.py:68
  30.1 14.3 %copy-start.2 = (bf16[64,2048]{1,0:T(8,128)(2,1)S(1)}, bf16[64,2048]{1,0:T(8,128)(2,1)}, u32[]{:S(2)}) copy-start(bf16[64,2048]{1,0:T(8,128)(2,1)} %param.9) | copy-start | bytes 786436
  79.3 16.5 %copy-start.1 = (bf16[256,2048]{1,0:T(8,128)(2,1)S(1)}, bf16[256,2048]{1,0:T(8,128)(2,1)}, u32[]{:S(2)}) copy-start(bf16[256,2048]{1,0:T(8,128)(2,1)} %all-gather.2.cloned.1.call-done) | copy-start | bytes 3145732
  90.3 44.1 %all-to-all-start.1 = ((bf16[8,4,32,128]{3,2,1,0:T(8,128)(2,1)}), bf16[8,4,32,128]{3,2,1,0:T(8,128)(2,1)S(1)}, u32[]{:S(2)}, u32[]{:S(2)}) async-start(bf16[8,4,32,128]{3,2,1,0:T(8,128)(2,1)} %bitcast.37), calls=%async_computation.1 | async-start | bytes 524288 | tf_op jit(solution)/shard_map/all_to_all | solution.py:89
Sparse Core Ops, SparseCore 0:
  45.9 15.0 all-gather.1
where the time goes:
time: 144 us
  blocking collectives  44.9 us (31%)
  other arithmetic  24.7 us (17%)
  waiting for transfers between devices  19.3 us (13%)
  matrix products  16.9 us (12%)
  between operations  14.2 us (10%)
  starting transfers between devices  12.9 us (9%)
  local copies, waits for them, and re-layouts  10.8 us (8%)
    psum x1, blocking collectives, body(): weight_grad = lax.psum(block_grad, 'rows') * grad_scale  37.6 us
    all_gather x1, waiting for transfers between devices, body(): portion = lax.all_gather(pre_grad, 'cols', axis=0, tiled=True)  14.7 us
    scatter-add x1, other arithmetic, body(): jax.ops.segment_sum(contrib_flat, self_target, num_segments=blocks_n + 1)  10.2 us
    scatter-add x1, other arithmetic, body(): jax.ops.segment_sum(contrib_flat, send_target, num_segments=slot_total + 1)  10.2 us
    all_gather x1, blocking collectives, body(): lax.all_gather(aggregated, 'cols', axis=0, tiled=True)  7.35 us
    all_to_all x1, starting transfers between devices, body(): lax.all_to_all(outgoing, 'rows', split_axis=0, concat_axis=0, tiled=True)  7.31 us
    dot_general x1, matrix products, body(): jnp.einsum('bkfj,bkij->fbi', picked, adj_weight, preferred_element_type=j...  6.91 us
    dot_general x1, matrix products, body(): jnp.einsum('fbi,bkij->bkfj', agg_grad.reshape(feat_rows, blocks_n, tile_n...  6.54 us
  transfers between devices with their start and end apart: 3, of which 2 were waited for; matrix products, arithmetic and copies ran while one was open for 4% of the time, Pallas kernels for 0%

commit v1 on v0

--- a/solution.py
+++ b/solution.py
@@ -65,7 +65,12 @@
         jnp.bfloat16
     )
     w_mine = lax.dynamic_slice_in_dim(weight, col_pos * feat_rows, feat_rows, 0)
-    portion = lax.all_gather(pre_grad, "cols", axis=0, tiled=True)
+    ring = [pre_grad]
+    for hop in range(3):
+        ring.append(lax.ppermute(ring[-1], "cols", [(dev, (dev + 1) % 4) for dev in range(4)]))
+    portion = jnp.roll(
+        jnp.concatenate(ring[::-1], axis=0), (lax.axis_index("cols") + 1) * ring[0].shape[0], axis=0
+    )
     grad_acc = jnp.dot(w_mine, portion, preferred_element_type=jnp.float32)
     block_grad = lax.dot_general(
         aggregated, portion, (((1,), (1,)), ((), ())), preferred_element_type=jnp.float32

time: 144 us -> 130 us (0.903)
  between operations: 14.2 us -> 0.93 us
  waiting for transfers between devices: 19.3 us -> 22.1 us
  starting transfers between devices: 12.9 us -> 11.3 us
    ppermute x0 -> x3, waiting for transfers between devices: none -> 16.6 us  [body(): lax.ppermute(ring[-1], 'cols', [(dev, (dev + 1) % 4) for dev in range(4)])]
    all_gather x1 -> x0, waiting for transfers between devices: 14.7 us -> none  [body(): portion = lax.all_gather(pre_grad, 'cols', axis=0, tiled=True)]
    all_to_all x1, starting transfers between devices: 5.52 us -> 3.59 us  [body(): lax.all_to_all(sending.astype(jnp.bfloat16), 'rows', split_axis=0, concat...]
  transfers between devices with their start and end apart: 3 -> 5, of which waited for: 2 -> 4; matrix products, arithmetic and copies ran while one was open for 4% -> 4% of each run, Pallas kernels for 0% -> 0%
where the time goes in v1:
time: 130 us; the launch traced here: 129 us
  blocking collectives  44.7 us (34%)
  other arithmetic  24.7 us (19%)
  waiting for transfers between devices  22.1 us (17%)
  matrix products  15.6 us (12%)
  starting transfers between devices  11.3 us (9%)
  local copies, waits for them, and re-layouts  10.1 us (8%)
    psum x1, blocking collectives, body(): weight_grad = lax.psum(block_grad, 'rows') * grad_scale  37.6 us
    ppermute x3, waiting for transfers between devices, body(): lax.ppermute(ring[-1], 'cols', [(dev, (dev + 1) % 4) for dev in range(4)])  16.6 us
    scatter-add x1, other arithmetic, body(): jax.ops.segment_sum(contrib_flat, self_target, num_segments=blocks_n + 1)  10.2 us
    scatter-add x1, other arithmetic, body(): jax.ops.segment_sum(contrib_flat, send_target, num_segments=slot_total + 1)  10.1 us
    all_to_all x1, starting transfers between devices, body(): lax.all_to_all(outgoing, 'rows', split_axis=0, concat_axis=0, tiled=True)  7.31 us
    all_gather x1, blocking collectives, body(): lax.all_gather(aggregated, 'cols', axis=0, tiled=True)  7.17 us
    dot_general x1, matrix products, body(): jnp.einsum('bkfj,bkij->fbi', picked, adj_weight, preferred_element_type=j...  6.91 us
    dot_general x1, matrix products, body(): jnp.einsum('fbi,bkij->bkfj', agg_grad.reshape(feat_rows, blocks_n, tile_n...  6.54 us
  transfers between devices with their start and end apart: 5, of which 4 were waited for; matrix products, arithmetic and copies ran while one was open for 4% of the time, Pallas kernels for 0%

profile of v1, /device:TPU:0, one launch (start us, length us, event | category | flops | bytes accessed | tf_op | source)
XLA Modules:
  0.0 129.3 jit_solution(928511400323275207)
XLA Ops:
  0.7 0.8 copy.41
  1.5 0.8 fusion.42
  3.3 0.9 copy.60
  4.5 0.7 copy.44
  5.2 7.3 %all-to-all-start = ((bf16[8,4,32,128]{3,2,1,0:T(8,128)(2,1)}), bf16[8,4,32,128]{3,2,1,0:T(8,128)(2,1)S(1)}, u32[]{:S(2)}, u32[]{:S(2)}) async-start(bf16[8,4,32,128]{3,2,1,0:T(8,128)(2,1)} %copy.44), calls=%async_computation | async-start | bytes 524288 | tf_op jit(solution)/shard_map/all_to_all | solution.py:47
  12.9 1.9 %gather_fusion = s32[256]{0:T(256)S(1)} fusion(s32[128]{0:T(128)S(1)} %sub.27, s32[1024]{0:T(1024)S(1)} %pad_clamp_fusion.2), kind=kCustom, calls=%fused_computation | custom fusion | bytes 3072 | tf_op jit(solution)/shard_map/gather | solution.py:39
  14.9 1.0 gather_fusion.2
  15.9 5.5 %all-to-all-done = bf16[8,4,32,128]{3,2,1,0:T(8,128)(2,1)S(1)} async-done(((bf16[8,4,32,128]{3,2,1,0:T(8,128)(2,1)}), bf16[8,4,32,128]{3,2,1,0:T(8,128)(2,1)S(1)}, u32[]{:S(2)}, u32[]{:S(2)}) %all-to-all-start) | async-done | bytes 262176 | tf_op jit(solution)/shard_map/all_to_all | solution.py:47
  21.4 2.2 %gather_fusion.1 = bf16[256,32,128]{2,1,0:T(8,128)(2,1)} fusion(bf16[32,32,128]{2,1,0:T(8,128)(2,1)S(1)} %bitcast.81, s32[1024]{0:T(1024)S(1)} %pad_clamp_fusion.1), kind=kCustom, calls=%fused_computation.1 | custom fusion | bytes 4195328 | tf_op jit(solution)/shard_map/gather | solution.py:48
  23.7 6.9 %fusion.16 = bf16[16,4,8,128]{3,2,1,0:T(8,128)(2,1)S(1)} fusion(bf16[16,16,128,128]{3,2,1,0:T(8,128)(2,1)} %param.7, bf16[16,16,32,128]{3,2,1,0:T(8,128)(2,1)} %bitcast.83, bf16[16,16,32,128]{3,2,1,0:T(8,128)(2,1)S(1)} %bitcast.82, pred[16,16]{1,0:T(8,128)(4,1)S(1)} %copy.40), kind=kOutput, calls=%fused_computation.20 | convolution fusion | flops 269549568 | bytes 12714240 | tf_op jit(solution)/shard_map/bkfj,bkij->fbi/dot_general | solution.py:53
  30.6 7.2 %all_gather.3 = bf16[128,2048]{1,0:T(8,128)(2,1)S(1)} all-gather(bf16[32,2048]{1,0:T(8,128)(2,1)S(1)} %bitcast.88), channel_id=1, replica_groups=mesh['rows'=8,'cols'=4] {'cols'}, dimensions={0}, use_global_device_ids=true | all-gather | bytes 655360 | tf_op jit(solution)/shard_map/all_gather | solution.py:58
  37.8 1.2 multiply_convert_fusion
  39.3 5.4 %collective-permute-done = bf16[64,2048]{1,0:T(8,128)(2,1)S(1)} collective-permute-done((bf16[64,2048]{1,0:T(8,128)(2,1)S(1)}, bf16[64,2048]{1,0:T(8,128)(2,1)S(1)}, u32[]{:S(2)}, u32[]{:S(2)}) %collective-permute-start) | collective-permute-done | bytes 262176 | tf_op jit(solution)/shard_map/ppermute | solution.py:70
  44.9 5.7 %collective-permute-done.1 = bf16[64,2048]{1,0:T(8,128)(2,1)S(1)} collective-permute-done((bf16[64,2048]{1,0:T(8,128)(2,1)S(1)}, bf16[64,2048]{1,0:T(8,128)(2,1)S(1)}, u32[]{:S(2)}, u32[]{:S(2)}) %collective-permute-start.1) | collective-permute-done | bytes 262176 | tf_op jit(solution)/shard_map/ppermute | solution.py:70
  50.9 5.5 %collective-permute-done.2 = bf16[64,2048]{1,0:T(8,128)(2,1)S(1)} collective-permute-done((bf16[64,2048]{1,0:T(8,128)(2,1)S(1)}, bf16[64,2048]{1,0:T(8,128)(2,1)S(1)}, u32[]{:S(2)}, u32[]{:S(2)}) %collective-permute-start.2) | collective-permute-done | bytes 262176 | tf_op jit(solution)/shard_map/ppermute | solution.py:70
  56.9 6.5 %fusion.31 = f32[16,32,16,128]{3,1,2,0:T(8,128)} fusion(bf16[16,16,128,128]{3,2,1,0:T(8,128)(2,1)} %param.7, bf16[32,16,128,1]{2,1,0,3:T(8,128)(2,1)S(1)} %bitcast.86), kind=kOutput, calls=%fused_computation.41 | convolution fusion | flops 268435456 | bytes 12713984 | tf_op jit(solution)/shard_map/fbi,bkij->bkfj/dot_general | solution.py:81
  63.5 10.2 %scatter_custom_fusion.2 = f32[17,4096]{1,0:T(8,128)S(1)} fusion(s32[256]{0:T(256)S(1)} %bitcast.97, f32[32,8,32,128]{3,2,1,0:T(8,128)} %bitcast.79, f32[]{:T(128)} %constant.90.clone.1), kind=kCustom, calls=%fused_computation.6 | custom fusion | flops 1048576 | bytes 4472836 | tf_op jit(solution)/shard_map/scatter-add | solution.py:106
  73.7 10.1 %scatter_custom_fusion = f32[33,4096]{1,0:T(8,128)S(1)} fusion(s32[256]{0:T(256)S(1)} %bitcast.96, f32[32,8,32,128]{3,2,1,0:T(8,128)} %bitcast.80, f32[]{:T(128)} %constant.90.clone.1), kind=kCustom, calls=%fused_computation.8 | custom fusion | flops 1048576 | bytes 4734980 | tf_op jit(solution)/shard_map/scatter-add | solution.py:90
  83.9 0.7 copy.63
  84.6 3.6 %all-to-all-start.1 = ((bf16[8,4,32,128]{3,2,1,0:T(8,128)(2,1)}), bf16[8,4,32,128]{3,2,1,0:T(8,128)(2,1)S(1)}, u32[]{:S(2)}, u32[]{:S(2)}) async-start(bf16[8,4,32,128]{3,2,1,0:T(8,128)(2,1)} %bitcast.37), calls=%async_computation.1 | async-start | bytes 524288 | tf_op jit(solution)/shard_map/all_to_all | solution.py:94
  88.6 37.6 %psum.7 = f32[32,256]{1,0:T(8,128)S(1)} all-reduce(f32[32,256]{1,0:T(8,128)S(1)} %fusion.20), channel_id=1, replica_groups=mesh['rows'=8,'cols'=4] {'rows'}, use_global_device_ids=true, to_apply=%region_4.5 | all-reduce | flops 8192 | bytes 65536 | tf_op jit(solution)/shard_map/psum | solution.py:79
  126.2 0.6 broadcast_multiply_fusion
  126.9 1.7 %scatter_custom_fusion.1 = f32[17,4096]{1,0:T(8,128)S(1)} fusion(s32[32]{0:T(128)S(1)} %reshape.376, f32[4,8,32,128]{3,2,1,0:T(8,128)S(1)} %bitcast_convert_fusion, f32[]{:T(128)} %constant.90.clone.1), kind=kCustom, calls=%fused_computation.24 | custom fusion | flops 131072 | bytes 802820 | tf_op jit(solution)/shard_map/scatter-add | solution.py:102
  128.6 0.7 copy.84
  (55 shorter events, 3.6 us)
Async XLA Ops:
  0.6 37.1 %copy-start = (bf16[128,256]{1,0:T(8,128)(2,1)S(1)}, bf16[128,256]{1,0:T(8,128)(2,1)}, u32[]{:S(2)}) copy-start(bf16[128,256]{1,0:T(8,128)(2,1)} %param.8) | copy-start | bytes 196612
  0.6 14.2 %copy-start.1 = (bf16[32,2048]{1,0:T(8,128)(2,1)S(1)}, bf16[32,2048]{1,0:T(8,128)(2,1)}, u32[]{:S(2)}) copy-start(bf16[32,2048]{1,0:T(8,128)(2,1)} %param.5) | copy-start | bytes 393220
  5.2 16.2 %all-to-all-start = ((bf16[8,4,32,128]{3,2,1,0:T(8,128)(2,1)}), bf16[8,4,32,128]{3,2,1,0:T(8,128)(2,1)S(1)}, u32[]{:S(2)}, u32[]{:S(2)}) async-start(bf16[8,4,32,128]{3,2,1,0:T(8,128)(2,1)} %copy.44), calls=%async_computation | async-start | bytes 524288 | tf_op jit(solution)/shard_map/all_to_all | solution.py:47
  23.7 14.1 %copy-start.2 = (bf16[64,2048]{1,0:T(8,128)(2,1)S(1)}, bf16[64,2048]{1,0:T(8,128)(2,1)}, u32[]{:S(2)}) copy-start(bf16[64,2048]{1,0:T(8,128)(2,1)} %param.9) | copy-start | bytes 786436
  39.0 5.8 %collective-permute-start = (bf16[64,2048]{1,0:T(8,128)(2,1)S(1)}, bf16[64,2048]{1,0:T(8,128)(2,1)S(1)}, u32[]{:S(2)}, u32[]{:S(2)}) collective-permute-start(bf16[64,2048]{1,0:T(8,128)(2,1)S(1)} %get-tuple-element.10), channel_id=1, source_target_pairs={{0,1},{1,2},{2,3},{3,0},{4,5},{5,6},{6,7},{7,4},{8,9},{9,10},{10,1... | collective-permute-start | bytes 786440 | tf_op jit(solution)/shard_map/ppermute | solution.py:70
  44.8 5.8 %collective-permute-start.1 = (bf16[64,2048]{1,0:T(8,128)(2,1)S(1)}, bf16[64,2048]{1,0:T(8,128)(2,1)S(1)}, u32[]{:S(2)}, u32[]{:S(2)}) collective-permute-start(bf16[64,2048]{1,0:T(8,128)(2,1)S(1)} %collective-permute-done), channel_id=1, source_target_pairs={{0,1},{1,2},{2,3},{3,0},{4,5},{5,6},{6,7},{7,4},{8,9},{9,10},{10,1... | collective-permute-start | bytes 786440 | tf_op jit(solution)/shard_map/ppermute | solution.py:70
  50.6 5.8 %collective-permute-start.2 = (bf16[64,2048]{1,0:T(8,128)(2,1)S(1)}, bf16[64,2048]{1,0:T(8,128)(2,1)S(1)}, u32[]{:S(2)}, u32[]{:S(2)}) collective-permute-start(bf16[64,2048]{1,0:T(8,128)(2,1)S(1)} %collective-permute-done.1), channel_id=1, source_target_pairs={{0,1},{1,2},{2,3},{3,0},{4,5},{5,6},{6,7},{7,4},{8,9},{9,10},{10,1... | collective-permute-start | bytes 786440 | tf_op jit(solution)/shard_map/ppermute | solution.py:70
  84.6 42.2 %all-to-all-start.1 = ((bf16[8,4,32,128]{3,2,1,0:T(8,128)(2,1)}), bf16[8,4,32,128]{3,2,1,0:T(8,128)(2,1)S(1)}, u32[]{:S(2)}, u32[]{:S(2)}) async-start(bf16[8,4,32,128]{3,2,1,0:T(8,128)(2,1)} %bitcast.37), calls=%async_computation.1 | async-start | bytes 524288 | tf_op jit(solution)/shard_map/all_to_all | solution.py:94
